TPU v7x, 256 devices: a whole 4x4x8 slice. The times are simulated.
256 devices in a mesh: tm: 8 (over z), height: 16 (over x, y), cam: 2 (over core).
Axes of the slice: x: 4, y: 4, z: 8, core: 2. Of those that a mesh axis runs over, the one named last changes fastest.
Arguments:
- video_clip: bfloat16 [2, 32, 128, 64, 256], P('cam', 'tm', 'height'), may hold values from -6 to 6
- valid_from: int32 [2], P('cam'), may hold values from 0 to 16, as said below
- norm_gain: float32 [256], replicated, may hold values from 0.5 to 1.5
- spatial_weight: bfloat16 [3, 3, 256, 256], replicated, may hold values from -0.125 to 0.125
- temporal_weight: bfloat16 [3, 256, 256], replicated, may hold values from -0.21875 to 0.21875
- mix_weight: bfloat16 [3, 256, 256], replicated, may hold values from -0.21875 to 0.21875
- cotangent: bfloat16 [2, 16, 128, 64, 256], P('cam', None, ('height', 'tm')), may hold values from -6 to 6
Outputs:
- encoded: bfloat16 [2, 16, 128, 64, 256], P('cam', None, ('height', 'tm'))
- video_gradient: bfloat16 [2, 32, 128, 64, 256], P('cam', 'tm', 'height')
- spatial_gradient: float32 [3, 3, 256, 256], replicated
- temporal_gradient: float32 [3, 256, 256], replicated
- mix_gradient: float32 [3, 256, 256], replicated
- gain_gradient: float32 [256], replicated
Inputs may be any that keep to these rules, and one draw needn't show every extreme that they name: Frames before valid_from of a camera are padding. In every draw some camera starts at 16.
All inputs are finite; a program needn't handle non-finite values.
Results may differ from a plain program's by a relative error of at most 0.0065.
Values may be sent and summed in bfloat16 or wider, within the bound.
A program may use at most 128 MiB of HBM per device.

v0:
```python
import functools
import math

import jax
import jax.numpy as jnp
from jax import lax
from jax.experimental import pallas as pl
from jax.experimental.pallas import tpu as pltpu
from jax.sharding import PartitionSpec as P

MESH = pl.DeviceIdType.MESH
BF = jnp.bfloat16
F32 = jnp.float32
LARGE = 12 * 256
SMALL = 4 * 256
VMEM_LIMIT = 46 << 20


class Place:
    def __init__(self):
        self.z = lax.axis_index("tm")
        self.h = lax.axis_index("height")
        self.c = lax.axis_index("cam")
        self.x = self.h // 4
        self.y = self.h % 4
        self.first = (1 - self.c) * self.x + self.c * self.y
        self.second = (1 - self.c) * self.y + self.c * self.x

    def across(self):
        return {"cam": 1 - self.c}

    def along_first(self, d):
        other = (self.first + d) % 4
        return {"height": (1 - self.c) * (other * 4 + self.y) + self.c * (self.x * 4 + other)}

    def along_second(self, d):
        other = (self.second + d) % 4
        return {"height": (1 - self.c) * (self.x * 4 + other) + self.c * (other * 4 + self.y)}

    def along_z(self, d):
        return {"tm": (self.z + d) % 8}


def remote(src, dst, send, recv, where):
    return pltpu.make_async_remote_copy(
        src_ref=src, dst_ref=dst, send_sem=send, recv_sem=recv, device_id=where, device_id_type=MESH
    )


def greet(peers):
    barrier = pltpu.get_barrier_semaphore()
    for peer in peers:
        pl.semaphore_signal(barrier, inc=1, device_id=peer, device_id_type=MESH)
    return barrier, len(peers)


def reduce_peers(place):
    return (
        [place.across()]
        + [place.along_first(d) for d in (1, 2, 3)]
        + [place.along_second(d) for d in (1, 2, 3)]
        + [place.along_z(d) for d in range(1, 8)]
    )


def block(ref, start, rows):
    return ref.at[pl.ds(pl.multiple_of(start, 16), rows)]


def started(copies):
    for copy in copies:
        copy.start()
    return copies


def finished(copies):
    for copy in copies:
        copy.wait()


class DeviceSum:
    def __init__(self, place, total, base, gathered, scratch):
        self.place, self.total, self.base, self.gathered = place, total, base, gathered
        (
            self.halved,
            self.landed_c,
            self.held_1,
            self.landed_1,
            self.held_2,
            self.landed_2,
            self.held_3,
            self.landed_3,
            self.placed_3,
        ) = scratch[:9]
        self.sems = scratch[9:]
        rows = gathered.shape[0]
        self.half, self.n1, self.n2, self.n3 = rows // 2, rows // 8, rows // 32, rows // 256
        self.mine = place.c * self.half
        self.at_1 = self.mine + place.first * self.n1
        self.at_2 = self.at_1 + place.second * self.n2

    def start_core(self):
        other = pl.multiple_of(self.base + (1 - self.place.c) * self.half, 16)
        self.halved[...] = self.total[pl.ds(other, self.half), :].astype(BF)
        s, r = self.sems[0], self.sems[1]
        self.pending = started([remote(self.halved, self.landed_c, s, r, self.place.across())])

    def start_first(self):
        finished(self.pending)
        own = pl.multiple_of(self.base + self.mine, 16)
        self.held_1[...] = (self.total[pl.ds(own, self.half), :] + self.landed_c[...].astype(F32)).astype(BF)
        s, r = self.sems[2], self.sems[3]
        self.pending = started(
            [
                remote(
                    block(self.held_1, (self.place.first + d) % 4 * self.n1, self.n1),
                    self.landed_1.at[d - 1],
                    s.at[d - 1],
                    r.at[d - 1],
                    self.place.along_first(d),
                )
                for d in (2, 1, 3)
            ]
        )

    def start_second(self):
        finished(self.pending)
        sum_here = self.held_1[pl.ds(pl.multiple_of(self.place.first * self.n1, 16), self.n1), :].astype(F32)
        for k in range(3):
            sum_here = sum_here + self.landed_1[k].astype(F32)
        self.held_2[...] = sum_here.astype(BF)
        s, r = self.sems[4], self.sems[5]
        self.pending = started(
            [
                remote(
                    block(self.held_2, (self.place.second + d) % 4 * self.n2, self.n2),
                    self.landed_2.at[d - 1],
                    s.at[d - 1],
                    r.at[d - 1],
                    self.place.along_second(d),
                )
                for d in (2, 1, 3)
            ]
        )

    def second_sum(self):
        finished(self.pending)
        sum_here = self.held_2[pl.ds(pl.multiple_of(self.place.second * self.n2, 16), self.n2), :].astype(F32)
        for k in range(3):
            sum_here = sum_here + self.landed_2[k].astype(F32)
        return sum_here

    def start_z(self):
        sum_here = self.second_sum()
        for k in range(8):
            self.held_3[k, 0 : self.n3] = sum_here[k * self.n3 : (k + 1) * self.n3].astype(BF)
        s, r = self.sems[6], self.sems[7]
        self.pending = started(
            [
                remote(
                    self.held_3.at[(self.place.z + d) % 8],
                    self.landed_3.at[d],
                    s.at[d],
                    r.at[d],
                    self.place.along_z(d),
                )
                for d in (4, 3, 5, 2, 6, 1, 7)
            ]
        )

    def start_z_back(self):
        finished(self.pending)
        z = self.place.z
        sum_here = self.held_3[z].astype(F32)
        for d in range(1, 8):
            sum_here = sum_here + self.landed_3[d].astype(F32)
        self.placed_3[z] = sum_here.astype(BF)
        s, r = self.sems[8], self.sems[9]
        self.pending = started(
            [
                remote(self.placed_3.at[z], self.placed_3.at[z], s.at[d], r.at[d], self.place.along_z(d))
                for d in (4, 3, 5, 2, 6, 1, 7)
            ]
        )

    def finish_z_back(self):
        finished(self.pending)
        pieces = [self.placed_3[k].astype(F32)[0 : self.n3] for k in range(8)]
        self.gathered[pl.ds(pl.multiple_of(self.at_2, 16), self.n2), :] = jnp.concatenate(pieces).astype(BF)

    def start_z_at_once(self):
        z = self.place.z
        self.landed_3[z] = self.second_sum().astype(BF)
        s, r = self.sems[6], self.sems[7]
        self.pending = started(
            [
                remote(self.landed_3.at[z], self.landed_3.at[z], s.at[d], r.at[d], self.place.along_z(d))
                for d in (4, 3, 5, 2, 6, 1, 7)
            ]
        )

    def finish_z_at_once(self):
        finished(self.pending)
        sum_here = self.landed_3[0].astype(F32)
        for k in range(1, 8):
            sum_here = sum_here + self.landed_3[k].astype(F32)
        self.gathered[pl.ds(pl.multiple_of(self.at_2, 16), self.n2), :] = sum_here.astype(BF)

    def start_second_back(self):
        at = block(self.gathered, self.at_2, self.n2)
        s, r = self.sems[10], self.sems[11]
        self.pending = started(
            [remote(at, at, s.at[d - 1], r.at[d - 1], self.place.along_second(d)) for d in (2, 1, 3)]
        )

    def start_first_back(self):
        finished(self.pending)
        at = block(self.gathered, self.at_1, self.n1)
        s, r = self.sems[12], self.sems[13]
        self.pending = started(
            [remote(at, at, s.at[d - 1], r.at[d - 1], self.place.along_first(d)) for d in (2, 1, 3)]
        )

    def start_core_back(self):
        finished(self.pending)
        at = block(self.gathered, self.mine, self.half)
        self.pending = started([remote(at, at, self.sems[14], self.sems[15], self.place.across())])

    def finish(self):
        finished(self.pending)


def sum_scratch(rows, at_once):
    dma, vmem = pltpu.SemaphoreType.DMA, pltpu.VMEM
    piece = rows // 32 if at_once else -(-rows // 256 // 16) * 16
    return [
        vmem((rows // 2, 256), BF),
        vmem((rows // 2, 256), BF),
        vmem((rows // 2, 256), BF),
        vmem((3, rows // 8, 256), BF),
        vmem((rows // 8, 256), BF),
        vmem((3, rows // 32, 256), BF),
        vmem((8, piece, 256), BF),
        vmem((8, piece, 256), BF),
        vmem((8, piece, 256), BF),
        dma,
        dma,
        *[dma((3,))] * 4,
        *[dma((8,))] * 4,
        *[dma((3,))] * 4,
        dma,
        dma,
    ]


def down(left, right):
    return lax.dot_general(left, right, (((1,), (0,)), ((), ())), preferred_element_type=F32)


def back(left, right):
    return lax.dot_general(left, right, (((1,), (1,)), ((), ())), preferred_element_type=F32)


def outer(left, right):
    return lax.dot_general(left, right, (((0,), (0,)), ((), ())), preferred_element_type=F32)


def flat(value):
    return value.reshape(-1, value.shape[-1])


def beside(rows):
    cells = rows.shape[0]
    column = lax.broadcasted_iota(jnp.int32, (cells, 256), 0) % 64
    left = jnp.where(column == 0, 0.0, pltpu.roll(rows, 1, 0))
    right = jnp.where(column == 63, 0.0, pltpu.roll(rows, cells - 1, 0))
    return left, right


def block_kernel(
    valid,
    gain_from,
    video,
    spatial_weight,
    temporal_weight,
    mix_weight,
    cotangent,
    enc,
    vg,
    gathered_large,
    gathered_small,
    xv,
    sw,
    swt,
    tw,
    mw,
    cv,
    edge_in,
    x3,
    slope,
    active,
    inverse,
    sg_rows,
    sg,
    strided,
    history,
    prior,
    g,
    g_edge,
    g3,
    total,
    gain,
    load_sems,
    edge_s,
    edge_r,
    a2a_s,
    a2a_r,
    next_s,
    next_r,
    prior_s,
    prior_r,
    st_s,
    st_r,
    ge_s,
    ge_r,
    *sum_scratches,
):
    place = Place()
    z, h = place.z, place.h
    above, below = {"height": (h + 15) % 16}, {"height": (h + 1) % 16}
    far = (4, 3, 5, 2, 6, 1, 7)

    loads = [
        pltpu.make_async_copy(cotangent, cv.at[pl.ds(0, 16)], load_sems.at[0]),
        pltpu.make_async_copy(mix_weight, mw, load_sems.at[1]),
        pltpu.make_async_copy(video, xv, load_sems.at[2]),
        pltpu.make_async_copy(spatial_weight, sw, load_sems.at[3]),
        pltpu.make_async_copy(temporal_weight, tw, load_sems.at[4]),
        pltpu.make_async_copy(gain_from, gain, load_sems.at[5]),
    ]
    for load in loads:
        load.start()
    barrier, count = greet(reduce_peers(place) + [above, below])

    cv[pl.ds(16, 2)] = jnp.zeros((2, 64, 256), BF)
    loads[0].wait()
    loads[1].wait()
    for f in (0, 8):
        rows = flat(cv[f : f + 8])
        sum_here = rows.astype(F32)
        for k in range(3):
            sum_here = sum_here + back(flat(cv[f + k : f + k + 8]), mw[k])
        sg_rows[f : f + 8] = sum_here.astype(BF).reshape(8, 64, 256)
    pl.semaphore_wait(barrier, count)

    edges = [
        remote(video.at[:, 7], edge_in.at[0], edge_s.at[0], edge_r.at[0], below),
        remote(video.at[:, 0], edge_in.at[1], edge_s.at[1], edge_r.at[1], above),
    ]
    for copy in edges:
        copy.start()
    a2a = {}
    for d in far:
        peer = (z + d) % 8
        a2a[d] = remote(
            sg_rows.at[pl.ds(2 * peer, 2)], sg.at[pl.ds(0, 2), z], a2a_s.at[d], a2a_r.at[d], place.along_z(d)
        )
        a2a[d].start()
    sg[pl.ds(0, 2), z] = sg_rows[pl.ds(2 * z, 2)]

    start = valid[0]
    loads[2].wait()
    loads[5].wait()
    for f in range(4):
        values = flat(xv[f]).astype(F32)
        values = jnp.where(z * 4 + f >= start, values, 0.0)
        scale = lax.rsqrt(jnp.mean(values * values, axis=-1, keepdims=True) + 1e-06)
        normed = values * scale * gain[...]
        left, right = beside(normed)
        inverse[:, f] = scale.reshape(8, 64, 1)
        x3[1:9, f, :, 0:256] = left.astype(BF).reshape(8, 64, 256)
        x3[1:9, f, :, 256:512] = normed.astype(BF).reshape(8, 64, 256)
        x3[1:9, f, :, 512:768] = right.astype(BF).reshape(8, 64, 256)

    loads[3].wait()

    def forward(row, rows):
        cells = rows * 256
        pre = down(x3[row : row + rows].reshape(cells, 768), sw[0])
        for i in (1, 2):
            pre = pre + down(x3[row + i : row + i + rows].reshape(cells, 768), sw[i])
        q = 1.0 / (1.0 + jnp.exp(-pre))
        active[row : row + rows] = (pre * q).astype(BF).reshape(rows, 4, 64, 256)
        slope[row : row + rows] = (q * (1.0 + pre * (1.0 - q))).reshape(rows, 4, 64, 256)

    forward(1, 2)
    forward(3, 2)
    forward(5, 2)
    frame = z * 4 + lax.broadcasted_iota(jnp.int32, (256, 256), 0) // 64
    for copy in edges:
        copy.wait()
    for side, row, inside in ((0, 0, h > 0), (1, 9, h < 15)):
        values = flat(edge_in[side]).astype(F32)
        values = jnp.where(frame >= start, values, 0.0)
        values = jnp.where(inside, values, 0.0)
        scale = lax.rsqrt(jnp.mean(values * values, axis=-1, keepdims=True) + 1e-06)
        normed = values * scale * gain[...]
        left, right = beside(normed)
        x3[row, :, :, 0:256] = left.astype(BF).reshape(4, 64, 256)
        x3[row, :, :, 256:512] = normed.astype(BF).reshape(4, 64, 256)
        x3[row, :, :, 512:768] = right.astype(BF).reshape(4, 64, 256)
    forward(0, 1)
    forward(7, 1)

    prior_copy = remote(active.at[:, 3], prior, prior_s, prior_r, place.along_z(1))
    prior_copy.start()
    history[pl.ds(0, 2)] = jnp.zeros((2, 64, 256), BF)
    loads[4].wait()
    st = {}

    def send_strided(s):
        for d in far:
            peer = (z + d) % 8
            st[s, d] = remote(
                strided.at[s, peer], history.at[2 + 2 * z + s], st_s.at[s, d], st_r.at[s, d], place.along_z(d)
            )
            st[s, d].start()
        history[2 + 2 * z + s] = strided[s, z]

    sum_here = down(flat(active[:, 3]), tw[0]) + down(flat(active[:, 2]), tw[1]) + down(flat(active[:, 1]), tw[2])
    strided[1] = sum_here.astype(BF).reshape(8, 64, 256)

    for i in range(3):
        for j in range(3):
            swt[i, j * 256 : (j + 1) * 256] = sw[i, j * 256 : (j + 1) * 256].T

    ahead = {0: remote(sg.at[0, z], sg.at[2, z], next_s.at[0], next_r.at[0], place.along_z(7))}
    ahead[0].start()
    for d in (1, 7, 2, 6, 3, 5, 4):
        a2a[d].wait()
        source = (z + 8 - d) % 8
        ahead[d] = remote(sg.at[0, source], sg.at[2, source], next_s.at[d], next_r.at[d], place.along_z(7))
        ahead[d].start()
    send_strided(1)


    def pre_gradient(f, active_gradient):
        value = (active_gradient * flat(slope[:, f])).astype(BF)
        g[:, f] = value.reshape(8, 64, 256)
        left, right = beside(value.astype(F32))
        g3[1:9, f, :, 0:256] = right.astype(BF).reshape(8, 64, 256)
        g3[1:9, f, :, 256:512] = value.reshape(8, 64, 256)
        g3[1:9, f, :, 512:768] = left.astype(BF).reshape(8, 64, 256)

    sg_0, sg_1 = flat(sg[0]), flat(sg[1])
    pre_gradient(0, back(sg_0, tw[1]))
    pre_gradient(1, back(sg_0, tw[0]) + back(sg_1, tw[2]))
    pre_gradient(2, back(sg_1, tw[1]))

    for i in range(3):
        total[i * 768 : (i + 1) * 768] = outer(x3[i : i + 8, 0:3].reshape(1536, 768), g[:, 0:3].reshape(1536, 256))
    base = 9 * 256
    total[base : base + 256] = outer(flat(active[:, 1]), sg_0) + outer(flat(active[:, 3]), sg_1)
    total[base + 256 : base + 512] = outer(flat(active[:, 0]), sg_0) + outer(flat(active[:, 2]), sg_1)

    prior_copy.wait()
    before = jnp.where(z > 0, flat(prior[...]).astype(F32), 0.0).astype(BF)
    sum_here = down(flat(active[:, 1]), tw[0]) + down(flat(active[:, 0]), tw[1]) + down(before, tw[2])
    strided[0] = sum_here.astype(BF).reshape(8, 64, 256)
    send_strided(0)

    for d in range(8):
        ahead[d].wait()
    sg_2 = jnp.where(z < 7, flat(sg[2]).astype(F32), 0.0).astype(BF)
    pre_gradient(3, back(sg_1, tw[0]) + back(sg_2, tw[2]))
    g_edges = started(
        [
            remote(g.at[7], g_edge.at[0], ge_s.at[0], ge_r.at[0], below),
            remote(g.at[0], g_edge.at[1], ge_s.at[1], ge_r.at[1], above),
        ]
    )

    for i in range(3):
        total[i * 768 : (i + 1) * 768] += outer(x3[i : i + 8, 3].reshape(512, 768), flat(g[:, 3]))
    total[base + 512 : base + 768] = outer(flat(active[:, 1]), sg_1) + outer(flat(active[:, 3]), sg_2)
    large = DeviceSum(place, total, 0, gathered_large, sum_scratches[:25])
    small = DeviceSum(place, total, LARGE, gathered_small, sum_scratches[25:])
    large.start_core()

    def clip_gradient(row, gain_sum):
        product = down(g3[row + 2 : row + 4].reshape(512, 768), swt[0])
        for i in (1, 2):
            product = product + down(g3[row + 2 - i : row + 4 - i].reshape(512, 768), swt[i])
        for k in range(2):
            grad = product[k * 256 : (k + 1) * 256]
            values = flat(xv[:, row + k]).astype(F32)
            values = jnp.where(frame >= start, values, 0.0)
            scale = inverse[row + k].reshape(256, 1)
            unit = values * scale
            gain_sum = gain_sum + jnp.sum(grad * unit, axis=0, keepdims=True)
            scaled = grad * gain[...]
            out = scale * (scaled - unit * jnp.mean(scaled * unit, axis=-1, keepdims=True))
            vg[:, row + k] = jnp.where(frame >= start, out, 0.0).astype(BF).reshape(4, 64, 256)
        return gain_sum

    gain_sum = jnp.zeros((1, 256), F32)
    gain_sum = clip_gradient(2, gain_sum)
    gain_sum = clip_gradient(4, gain_sum)
    large.start_first()
    finished(g_edges)
    for side, row, inside in ((0, 0, h > 0), (1, 9, h < 15)):
        values = flat(g_edge[side]).astype(F32)
        values = jnp.where(inside, values, 0.0)
        left, right = beside(values)
        g3[row, :, :, 0:256] = right.astype(BF).reshape(4, 64, 256)
        g3[row, :, :, 256:512] = values.astype(BF).reshape(4, 64, 256)
        g3[row, :, :, 512:768] = left.astype(BF).reshape(4, 64, 256)
    gain_sum = clip_gradient(0, gain_sum)
    gain_sum = clip_gradient(6, gain_sum)
    total[15 * 256 : 16 * 256] = jnp.zeros((256, 256), F32)
    total[15 * 256 : 15 * 256 + 1] = gain_sum

    for s in (1, 0):
        for d in far:
            st[s, d].wait()
    base = 12 * 256
    cot_all = flat(cv[0:16])
    for k in range(3):
        total[base + k * 256 : base + (k + 1) * 256] = outer(flat(history[2 - k : 18 - k]), cot_all)
    small.start_core()
    large.start_second()
    for f in (0, 8):
        sum_here = flat(history[f + 2 : f + 10]).astype(F32)
        for k in range(3):
            sum_here = sum_here + down(flat(history[f + 2 - k : f + 10 - k]), mw[k])
        enc[f : f + 8] = sum_here.astype(BF).reshape(8, 64, 256)
    small.start_first()
    large.start_z()
    small.start_second()
    large.start_z_back()
    small.start_z_at_once()
    large.finish_z_back()
    large.start_second_back()
    small.finish_z_at_once()
    small.start_second_back()
    large.start_first_back()
    small.start_first_back()
    small.start_core_back()
    large.start_core_back()
    small.finish()
    large.finish()


def finish_kernel(scale, enc, vg, large, small, encoded, video_gradient, spatial, temporal, mix, gain_out, ws, wt, wm, wg, sems):
    copies = started(
        [
            pltpu.make_async_copy(vg, video_gradient, sems.at[0]),
            pltpu.make_async_copy(enc, encoded, sems.at[1]),
        ]
    )
    for i in range(9):
        ws[i] = large[i * 256 : (i + 1) * 256].astype(F32) * scale
    copies += started([pltpu.make_async_copy(ws, spatial, sems.at[2])])
    for i in range(3):
        wt[i] = large[(9 + i) * 256 : (10 + i) * 256].astype(F32) * scale
        wm[i] = small[i * 256 : (i + 1) * 256].astype(F32) * scale
    wg[...] = small[3 * 256 : 3 * 256 + 16].astype(F32)[0:1] * scale
    copies += started(
        [
            pltpu.make_async_copy(wt, temporal, sems.at[3]),
            pltpu.make_async_copy(wm, mix, sems.at[4]),
            pltpu.make_async_copy(wg, gain_out, sems.at[5]),
        ]
    )
    finished(copies)


def block_call(valid, gain, video, spatial_weight, temporal_weight, mix_weight, cotangent):
    vmem, dma = pltpu.VMEM, pltpu.SemaphoreType.DMA
    anywhere = pl.BlockSpec(memory_space=pltpu.HBM)
    here = pl.BlockSpec(memory_space=pltpu.VMEM)
    parts = pl.pallas_call(
        block_kernel,
        out_shape=(
            jax.ShapeDtypeStruct((16, 64, 256), BF),
            jax.ShapeDtypeStruct((4, 8, 64, 256), BF),
            jax.ShapeDtypeStruct((LARGE, 256), BF),
            jax.ShapeDtypeStruct((SMALL, 256), BF),
        ),
        in_specs=[pl.BlockSpec(memory_space=pltpu.SMEM)] + [anywhere] * 6,
        out_specs=(here,) * 4,
        scratch_shapes=[
            vmem((4, 8, 64, 256), BF),
            vmem((3, 768, 256), BF),
            vmem((3, 768, 256), BF),
            vmem((3, 256, 256), BF),
            vmem((3, 256, 256), BF),
            vmem((18, 64, 256), BF),
            vmem((2, 4, 64, 256), BF),
            vmem((10, 4, 64, 768), BF),
            vmem((8, 4, 64, 256), F32),
            vmem((8, 4, 64, 256), BF),
            vmem((8, 4, 64, 1), F32),
            vmem((16, 64, 256), BF),
            vmem((3, 8, 64, 256), BF),
            vmem((2, 8, 64, 256), BF),
            vmem((18, 64, 256), BF),
            vmem((8, 64, 256), BF),
            vmem((8, 4, 64, 256), BF),
            vmem((2, 4, 64, 256), BF),
            vmem((10, 4, 64, 768), BF),
            vmem((LARGE + SMALL, 256), F32),
            vmem((1, 256), F32),
            dma((6,)),
            dma((2,)),
            dma((2,)),
            dma((8,)),
            dma((8,)),
            dma((8,)),
            dma((8,)),
            dma,
            dma,
            dma((2, 8)),
            dma((2, 8)),
            dma((2,)),
            dma((2,)),
        ]
        + sum_scratch(LARGE, False)
        + sum_scratch(SMALL, True),
        compiler_params=pltpu.CompilerParams(collective_id=0, has_side_effects=True, vmem_limit_bytes=VMEM_LIMIT),
        name="down_block",
    )(
        valid,
        *[
            pltpu.with_memory_space_constraint(array, pltpu.HBM)
            for array in (gain, video, spatial_weight, temporal_weight, mix_weight, cotangent)
        ],
    )
    scale = 1.0 / math.sqrt(2 * 32 * 128 * 64)
    return pl.pallas_call(
        functools.partial(finish_kernel, scale),
        out_shape=(
            jax.ShapeDtypeStruct((16, 64, 256), BF),
            jax.ShapeDtypeStruct((4, 8, 64, 256), BF),
            jax.ShapeDtypeStruct((9, 256, 256), F32),
            jax.ShapeDtypeStruct((3, 256, 256), F32),
            jax.ShapeDtypeStruct((3, 256, 256), F32),
            jax.ShapeDtypeStruct((1, 256), F32),
        ),
        in_specs=[here] * 4,
        out_specs=(anywhere,) * 6,
        scratch_shapes=[
            vmem((9, 256, 256), F32),
            vmem((3, 256, 256), F32),
            vmem((3, 256, 256), F32),
            vmem((1, 256), F32),
            dma((6,)),
        ],
        compiler_params=pltpu.CompilerParams(vmem_limit_bytes=12 << 20),
        name="write_out",
    )(*parts)


def on_device(video_clip, valid_from, norm_gain, spatial_weight, temporal_weight, mix_weight, cotangent):
    encoded, video_gradient, spatial, temporal, mix, gain = block_call(
        valid_from,
        norm_gain.reshape(1, 256),
        video_clip.reshape(4, 8, 64, 256),
        spatial_weight.reshape(3, 768, 256),
        temporal_weight,
        mix_weight,
        cotangent.reshape(16, 64, 256),
    )
    return (
        encoded.reshape(1, 16, 1, 64, 256),
        video_gradient.reshape(1, 4, 8, 64, 256),
        spatial.reshape(3, 3, 256, 256),
        temporal,
        mix,
        gain.reshape(256),
    )


def solution(mesh):
    return jax.shard_map(
        on_device,
        mesh=mesh,
        in_specs=(
            P("cam", "tm", "height", None, None),
            P("cam"),
            P(),
            P(),
            P(),
            P(),
            P("cam", None, ("height", "tm"), None, None),
        ),
        out_specs=(
            P("cam", None, ("height", "tm"), None, None),
            P("cam", "tm", "height", None, None),
            P(),
            P(),
            P(),
            P(),
        ),
        check_vma=False,
    )
```

profile of v0, /device:TPU:1, one launch (start us, length us, event | category | flops | bytes accessed | tf_op | source)
XLA Modules:
  0.0 86.3 jit_solution(14837609415011162928)
XLA Ops:
  1.3 82.4 %down_block.1 = (bf16[16,64,256]{2,1,0:T(8,128)(2,1)S(1)}, bf16[4,8,64,256]{3,2,1,0:T(8,128)(2,1)S(1)}, bf16[3072,256]{1,0:T(8,128)(2,1)S(1)}, bf16[1024,256]{1,0:T(8,128)(2,1)S(1)}) custom-call(s32[1]{0:T(128)S(6)} %copy.14.valid, f32[1,256]{1,0:T(1,128)} %bitcast.13, bf16[4,8,64,256]{3,2,1,0:T(8,128)(2,1)} %bitcast.11, bf16[3,768,256]{2,1,0:T(8,128)(2,1)} %bitcast.10, ...), custom_call_target="tpu_custom_call" | custom-call | tf_op jit(solution)/shard_map/down_block/pallas_call | solution.py:582
  83.7 2.5 %write_out.1 = (bf16[16,64,256]{2,1,0:T(8,128)(2,1)}, bf16[4,8,64,256]{3,2,1,0:T(8,128)(2,1)}, f32[9,256,256]{2,1,0:T(8,128)}, f32[3,256,256]{2,1,0:T(8,128)}, f32[3,256,256]{2,1,0:T(8,128)}, /*index=5*/f32[1,256]{1,0:T(1,128)}) custom-call(bf16[16,64,256]{2,1,0:T(8,128)(2,1)S(1)} %get-tuple-element.16.enc, ...), custom_call_target="tpu_custom_call" | custom-call | tf_op jit(solution)/shard_map/write_out/pallas_call | solution.py:640
where the time goes:
time: 86.4 us; the launch traced here: 86.3 us
  Pallas kernels  84.9 us (98%)
  between operations  1.45 us (2%)
    pallas_call x1, Pallas kernels, block_call(): pl.pallas_call(block_kernel, out_shape=(jax.ShapeDtypeStruct((16, 64, 256...  82.4 us
    pallas_call x1, Pallas kernels, block_call(): pl.pallas_call(functools.partial(finish_kernel, scale), out_shape=(jax.Sh...  2.49 us

commit v1 on v0

--- a/solution.py
+++ b/solution.py
@@ -37,6 +37,15 @@
         other = (self.second + d) % 4
         return {"height": (1 - self.c) * (self.x * 4 + other) + self.c * (other * 4 + self.y)}
 
+    def along_x(self, d):
+        return {"height": (self.x + d) % 4 * 4 + self.y}
+
+    def along_y(self, d):
+        return {"height": self.x * 4 + (self.y + d) % 4}
+
+    def in_plane(self, d):
+        return {"height": (self.h + d) % 16}
+
     def along_z(self, d):
         return {"tm": (self.z + d) % 8}
 
@@ -55,12 +64,7 @@
 
 
 def reduce_peers(place):
-    return (
-        [place.across()]
-        + [place.along_first(d) for d in (1, 2, 3)]
-        + [place.along_second(d) for d in (1, 2, 3)]
-        + [place.along_z(d) for d in range(1, 8)]
-    )
+    return [place.across()] + [place.in_plane(d) for d in range(1, 16)] + [place.along_z(d) for d in range(1, 8)]
 
 
 def block(ref, start, rows):
@@ -76,6 +80,21 @@
 def finished(copies):
     for copy in copies:
         copy.wait()
+
+
+ORDER = (2, 1, 3, 0)
+UP = (2, 1)
+BACK_ORDER = (0, 1, 3, 2)
+FAR_FIRST = (4, 3, 5, 2, 6, 1, 7)
+PLANE = (10, 5, 15, 7, 13, 9, 11, 6, 14, 8, 2, 12, 4, 3, 1)
+
+
+def await_bytes(ref, sem):
+    pltpu.make_async_copy(ref, ref, sem).wait()
+
+
+def kind_of(group, e):
+    return (2, 3 if e in UP else 1, 1 if e in UP else 3, 0)[group]
 
 
 class DeviceSum:
@@ -88,169 +107,302 @@
             self.landed_1,
             self.held_2,
             self.landed_2,
+            self.own_2,
             self.held_3,
             self.landed_3,
             self.placed_3,
-        ) = scratch[:9]
-        self.sems = scratch[9:]
+            self.sent,
+            self.core_r,
+            self.first_r,
+            self.second_r,
+            self.z_r,
+            self.second_back_r,
+            self.first_back_r,
+            self.core_back_r,
+        ) = scratch
         rows = gathered.shape[0]
         self.half, self.n1, self.n2, self.n3 = rows // 2, rows // 8, rows // 32, rows // 256
         self.mine = place.c * self.half
-        self.at_1 = self.mine + place.first * self.n1
-        self.at_2 = self.at_1 + place.second * self.n2
-
-    def start_core(self):
-        other = pl.multiple_of(self.base + (1 - self.place.c) * self.half, 16)
-        self.halved[...] = self.total[pl.ds(other, self.half), :].astype(BF)
-        s, r = self.sems[0], self.sems[1]
-        self.pending = started([remote(self.halved, self.landed_c, s, r, self.place.across())])
-
-    def start_first(self):
-        finished(self.pending)
-        own = pl.multiple_of(self.base + self.mine, 16)
-        self.held_1[...] = (self.total[pl.ds(own, self.half), :] + self.landed_c[...].astype(F32)).astype(BF)
-        s, r = self.sems[2], self.sems[3]
-        self.pending = started(
-            [
-                remote(
-                    block(self.held_1, (self.place.first + d) % 4 * self.n1, self.n1),
-                    self.landed_1.at[d - 1],
-                    s.at[d - 1],
-                    r.at[d - 1],
-                    self.place.along_first(d),
-                )
-                for d in (2, 1, 3)
-            ]
-        )
-
-    def start_second(self):
-        finished(self.pending)
-        sum_here = self.held_1[pl.ds(pl.multiple_of(self.place.first * self.n1, 16), self.n1), :].astype(F32)
-        for k in range(3):
-            sum_here = sum_here + self.landed_1[k].astype(F32)
-        self.held_2[...] = sum_here.astype(BF)
-        s, r = self.sems[4], self.sems[5]
-        self.pending = started(
-            [
-                remote(
-                    block(self.held_2, (self.place.second + d) % 4 * self.n2, self.n2),
-                    self.landed_2.at[d - 1],
-                    s.at[d - 1],
-                    r.at[d - 1],
-                    self.place.along_second(d),
-                )
-                for d in (2, 1, 3)
-            ]
-        )
-
-    def second_sum(self):
-        finished(self.pending)
-        sum_here = self.held_2[pl.ds(pl.multiple_of(self.place.second * self.n2, 16), self.n2), :].astype(F32)
-        for k in range(3):
-            sum_here = sum_here + self.landed_2[k].astype(F32)
-        return sum_here
+
+    def rows(self, start):
+        return pl.ds(pl.multiple_of(start, 16), self.n2)
+
+    def piece(self, d, e):
+        place = self.place
+        return self.mine + (place.first + d) % 4 * self.n1 + (place.second + e) % 4 * self.n2
+
+    def send_core(self):
+        place = self.place
+        other = self.base + (1 - place.c) * self.half
+        for group in range(4):
+            for i, e in enumerate(ORDER):
+                d = kind_of(group, e)
+                at = other + (place.second + d) % 4 * self.n1 + (place.first + e) % 4 * self.n2
+                self.halved[group * 4 + i] = self.total[self.rows(at), :].astype(BF)
+        for group in range(4):
+            four = pl.ds(group * 4, 4)
+            remote(
+                self.halved.at[four], self.landed_c.at[four], self.sent.at[0], self.core_r.at[group], place.across()
+            ).start()
+
+    def await_core(self, group):
+        await_bytes(self.landed_c.at[pl.ds(group * 4, 4)], self.core_r.at[group])
+
+    def chip_sum(self, group, i, e):
+        at = self.base + self.piece(kind_of(group, e), e)
+        return self.total[self.rows(at), :] + self.landed_c[group * 4 + i].astype(F32)
+
+    def send_held(self, group, i, value, d):
+        k = group * 4 + i
+        self.held_1[k] = value.astype(BF)
+        remote(
+            self.held_1.at[k],
+            self.landed_1.at[k],
+            self.sent.at[1],
+            self.first_r.at[group],
+            self.place.along_first(d),
+        ).start()
+
+    def send_first(self):
+        self.await_core(0)
+        for i, e in enumerate(ORDER):
+            self.send_held(0, i, self.chip_sum(0, i, e), 1 if e in UP else 3)
+        self.await_core(1)
+        for i, e in enumerate(ORDER):
+            self.send_held(1, i, self.chip_sum(1, i, e), kind_of(1, e))
+
+    def relay_first(self):
+        self.await_core(2)
+        await_bytes(self.landed_1.at[pl.ds(0, 4)], self.first_r.at[0])
+        for i, e in enumerate(ORDER):
+            self.send_held(2, i, self.chip_sum(2, i, e) + self.landed_1[i].astype(F32), kind_of(2, e))
+
+    def send_second(self):
+        self.await_core(3)
+        for group in (1, 2):
+            await_bytes(self.landed_1.at[pl.ds(group * 4, 4)], self.first_r.at[group])
+        for i, e in enumerate(ORDER):
+            sum_here = self.chip_sum(3, i, e)
+            sum_here = sum_here + self.landed_1[4 + i].astype(F32) + self.landed_1[8 + i].astype(F32)
+            if e == 0:
+                self.own_2[...] = sum_here
+                continue
+            self.held_2[e - 1] = sum_here.astype(BF)
+            remote(
+                self.held_2.at[e - 1],
+                self.landed_2.at[e - 1],
+                self.sent.at[2],
+                self.second_r,
+                self.place.along_second(e),
+            ).start()
 
     def start_z(self):
-        sum_here = self.second_sum()
+        await_bytes(self.landed_2, self.second_r)
+        sum_here = self.own_2[...]
+        for e in (1, 2, 3):
+            sum_here = sum_here + self.landed_2[e - 1].astype(F32)
         for k in range(8):
             self.held_3[k, 0 : self.n3] = sum_here[k * self.n3 : (k + 1) * self.n3].astype(BF)
-        s, r = self.sems[6], self.sems[7]
-        self.pending = started(
-            [
-                remote(
-                    self.held_3.at[(self.place.z + d) % 8],
-                    self.landed_3.at[d],
-                    s.at[d],
-                    r.at[d],
-                    self.place.along_z(d),
-                )
-                for d in (4, 3, 5, 2, 6, 1, 7)
-            ]
-        )
+        for d in FAR_FIRST:
+            remote(
+                self.held_3.at[(self.place.z + d) % 8],
+                self.landed_3.at[d - 1],
+                self.sent.at[3],
+                self.z_r.at[0],
+                self.place.along_z(d),
+            ).start()
 
     def start_z_back(self):
-        finished(self.pending)
+        await_bytes(self.landed_3, self.z_r.at[0])
         z = self.place.z
         sum_here = self.held_3[z].astype(F32)
         for d in range(1, 8):
-            sum_here = sum_here + self.landed_3[d].astype(F32)
+            sum_here = sum_here + self.landed_3[d - 1].astype(F32)
         self.placed_3[z] = sum_here.astype(BF)
-        s, r = self.sems[8], self.sems[9]
-        self.pending = started(
-            [
-                remote(self.placed_3.at[z], self.placed_3.at[z], s.at[d], r.at[d], self.place.along_z(d))
-                for d in (4, 3, 5, 2, 6, 1, 7)
-            ]
+        for d in FAR_FIRST:
+            remote(
+                self.placed_3.at[z], self.placed_3.at[z], self.sent.at[4], self.z_r.at[1], self.place.along_z(d)
+            ).start()
+
+    def start_back(self):
+        await_bytes(self.landed_3, self.z_r.at[1])
+        pieces = [self.placed_3[k].astype(F32)[0 : self.n3] for k in range(8)]
+        self.gathered[self.rows(self.piece(0, 0)), :] = jnp.concatenate(pieces).astype(BF)
+        for d in (2, 1, 3):
+            self.copy_back(self.piece(0, 0), 5, self.second_back_r.at[d // 2 if d == 2 else 0], self.place.along_second(d))
+        self.hand_on(0)
+
+    def copy_back(self, start, sent, received, where):
+        at = self.gathered.at[self.rows(start)]
+        remote(at, at, self.sent.at[sent], received, where).start()
+
+    def hand_on(self, e):
+        for d in (1, 3):
+            self.copy_back(self.piece(0, 4 - e), 6, self.first_back_r.at[e], self.place.along_first(d))
+        self.copy_back(self.piece(0, 4 - e), 7, self.core_back_r, self.place.across())
+
+    def back_second(self, which):
+        await_bytes(self.landed_2.at[pl.ds(0, 2 - which)], self.second_back_r.at[which])
+        for e in ((1, 3), (2,))[which]:
+            self.hand_on(e)
+
+    def back_first(self, e):
+        await_bytes(self.landed_1.at[pl.ds(0, 2)], self.first_back_r.at[e])
+        for d in (1, 3):
+            at = self.piece(4 - d, 4 - e)
+            if d == (1 if e in UP else 3):
+                self.copy_back(at, 6, self.first_back_r.at[4], self.place.along_first(d))
+            self.copy_back(at, 7, self.core_back_r, self.place.across())
+
+    def back_far(self):
+        await_bytes(self.landed_1.at[pl.ds(0, 4)], self.first_back_r.at[4])
+        for e in BACK_ORDER:
+            self.copy_back(self.piece(2, 4 - e), 7, self.core_back_r, self.place.across())
+
+    def finish(self):
+        await_bytes(self.landed_c, self.core_back_r)
+        for k, ref in enumerate(
+            (
+                self.halved,
+                self.held_1,
+                self.held_2,
+                self.landed_3,
+                self.landed_3,
+                self.held_2,
+                self.held_1,
+                self.halved,
+            )
+        ):
+            await_bytes(ref, self.sent.at[k])
+
+
+class PlaneSum:
+    def __init__(self, place, total, base, gathered, scratch):
+        self.place, self.total, self.base, self.gathered = place, total, base, gathered
+        self.halved, self.landed_c, self.held, self.landed, self.landed_z, self.sent, self.received = scratch
+        rows = gathered.shape[0]
+        self.half, self.n = rows // 2, rows // 32
+        self.mine = place.c * self.half
+
+    def send_core(self):
+        other = pl.multiple_of(self.base + (1 - self.place.c) * self.half, 16)
+        self.halved[...] = self.total[pl.ds(other, self.half), :].astype(BF)
+        remote(self.halved, self.landed_c, self.sent.at[0], self.received.at[0], self.place.across()).start()
+
+    def send_plane(self):
+        await_bytes(self.landed_c, self.received.at[0])
+        own = pl.multiple_of(self.base + self.mine, 16)
+        value = self.total[pl.ds(own, self.half), :] + self.landed_c[...].astype(F32)
+        self.held[...] = value.astype(BF).reshape(16, self.n, 256)
+        for d in PLANE:
+            remote(
+                self.held.at[(self.place.h + d) % 16],
+                self.landed.at[d - 1],
+                self.sent.at[1],
+                self.received.at[1],
+                self.place.in_plane(d),
+            ).start()
+
+    def start_z(self):
+        await_bytes(self.landed, self.received.at[1])
+        sum_here = self.held[self.place.h].astype(F32)
+        for k in range(15):
+            sum_here = sum_here + self.landed[k].astype(F32)
+        z = self.place.z
+        self.landed_z[z] = sum_here.astype(BF)
+        for d in FAR_FIRST:
+            remote(
+                self.landed_z.at[z], self.landed_z.at[z], self.sent.at[2], self.received.at[2], self.place.along_z(d)
+            ).start()
+
+    def start_back(self):
+        await_bytes(self.landed_z.at[pl.ds(0, 7)], self.received.at[2])
+        sum_here = self.landed_z[0].astype(F32)
+        for k in range(1, 8):
+            sum_here = sum_here + self.landed_z[k].astype(F32)
+        rows = pl.ds(pl.multiple_of(self.mine + self.place.h * self.n, 16), self.n)
+        self.gathered[rows, :] = sum_here.astype(BF)
+        at = self.gathered.at[rows]
+        for d in PLANE:
+            remote(at, at, self.sent.at[3], self.received.at[3], self.place.in_plane(d)).start()
+
+    def core_back(self):
+        await_bytes(self.landed, self.received.at[3])
+        at = self.gathered.at[pl.ds(pl.multiple_of(self.mine, 16), self.half)]
+        remote(at, at, self.sent.at[4], self.received.at[4], self.place.across()).start()
+
+    def finish(self):
+        await_bytes(self.landed_c, self.received.at[4])
+        for k, ref in enumerate((self.halved, self.landed, self.landed_z.at[pl.ds(0, 7)], self.landed, self.halved)):
+            await_bytes(ref, self.sent.at[k])
+
+
+class RowSum:
+    def __init__(self, place, scratch):
+        self.place = place
+        self.slots, self.sent, self.received = scratch[:4], scratch[4], scratch[5]
+        self.at = (place.c, place.x, place.y, place.z)
+        self.peers = (
+            [place.across()],
+            [place.along_x(d) for d in (1, 2, 3)],
+            [place.along_y(d) for d in (1, 2, 3)],
+            [place.along_z(d) for d in range(1, 8)],
         )
 
-    def finish_z_back(self):
-        finished(self.pending)
-        pieces = [self.placed_3[k].astype(F32)[0 : self.n3] for k in range(8)]
-        self.gathered[pl.ds(pl.multiple_of(self.at_2, 16), self.n2), :] = jnp.concatenate(pieces).astype(BF)
-
-    def start_z_at_once(self):
-        z = self.place.z
-        self.landed_3[z] = self.second_sum().astype(BF)
-        s, r = self.sems[6], self.sems[7]
-        self.pending = started(
-            [
-                remote(self.landed_3.at[z], self.landed_3.at[z], s.at[d], r.at[d], self.place.along_z(d))
-                for d in (4, 3, 5, 2, 6, 1, 7)
-            ]
-        )
-
-    def finish_z_at_once(self):
-        finished(self.pending)
-        sum_here = self.landed_3[0].astype(F32)
-        for k in range(1, 8):
-            sum_here = sum_here + self.landed_3[k].astype(F32)
-        self.gathered[pl.ds(pl.multiple_of(self.at_2, 16), self.n2), :] = sum_here.astype(BF)
-
-    def start_second_back(self):
-        at = block(self.gathered, self.at_2, self.n2)
-        s, r = self.sems[10], self.sems[11]
-        self.pending = started(
-            [remote(at, at, s.at[d - 1], r.at[d - 1], self.place.along_second(d)) for d in (2, 1, 3)]
-        )
-
-    def start_first_back(self):
-        finished(self.pending)
-        at = block(self.gathered, self.at_1, self.n1)
-        s, r = self.sems[12], self.sems[13]
-        self.pending = started(
-            [remote(at, at, s.at[d - 1], r.at[d - 1], self.place.along_first(d)) for d in (2, 1, 3)]
-        )
-
-    def start_core_back(self):
-        finished(self.pending)
-        at = block(self.gathered, self.mine, self.half)
-        self.pending = started([remote(at, at, self.sems[14], self.sems[15], self.place.across())])
-
-    def finish(self):
-        finished(self.pending)
-
-
-def sum_scratch(rows, at_once):
+    def send(self, stage, value):
+        slots, at = self.slots[stage], self.at[stage]
+        slots[at] = value
+        for peer in self.peers[stage]:
+            remote(slots.at[at], slots.at[at], self.sent.at[stage], self.received.at[stage], peer).start()
+
+    def take(self, stage):
+        slots = self.slots[stage]
+        others = slots.at[pl.ds(0, slots.shape[0] - 1)]
+        await_bytes(others, self.received.at[stage])
+        await_bytes(others, self.sent.at[stage])
+        value = slots[0]
+        for k in range(1, slots.shape[0]):
+            value = value + slots[k]
+        return value
+
+    def step(self, stage):
+        self.send(stage + 1, self.take(stage))
+
+
+def sum_scratch():
     dma, vmem = pltpu.SemaphoreType.DMA, pltpu.VMEM
-    piece = rows // 32 if at_once else -(-rows // 256 // 16) * 16
-    return [
-        vmem((rows // 2, 256), BF),
-        vmem((rows // 2, 256), BF),
-        vmem((rows // 2, 256), BF),
-        vmem((3, rows // 8, 256), BF),
-        vmem((rows // 8, 256), BF),
-        vmem((3, rows // 32, 256), BF),
-        vmem((8, piece, 256), BF),
-        vmem((8, piece, 256), BF),
-        vmem((8, piece, 256), BF),
+    n2, n = LARGE // 32, SMALL // 32
+    large = [
+        vmem((16, n2, 256), BF),
+        vmem((16, n2, 256), BF),
+        vmem((12, n2, 256), BF),
+        vmem((12, n2, 256), BF),
+        vmem((3, n2, 256), BF),
+        vmem((3, n2, 256), BF),
+        vmem((n2, 256), F32),
+        vmem((8, 16, 256), BF),
+        vmem((7, 16, 256), BF),
+        vmem((8, 16, 256), BF),
+        dma((8,)),
+        dma((4,)),
+        dma((3,)),
         dma,
-        dma,
-        *[dma((3,))] * 4,
-        *[dma((8,))] * 4,
-        *[dma((3,))] * 4,
-        dma,
+        dma((2,)),
+        dma((2,)),
+        dma((5,)),
         dma,
     ]
+    small = [
+        vmem((SMALL // 2, 256), BF),
+        vmem((SMALL // 2, 256), BF),
+        vmem((16, n, 256), BF),
+        vmem((15, n, 256), BF),
+        vmem((8, n, 256), BF),
+        dma((5,)),
+        dma((5,)),
+    ]
+    row = [vmem((k, 8, 256), F32) for k in (2, 4, 4, 8)] + [dma((4,)), dma((4,))]
+    return large, small, row
 
 
 def down(left, right):
@@ -289,6 +441,7 @@
     vg,
     gathered_large,
     gathered_small,
+    gain_total,
     xv,
     sw,
     swt,
@@ -323,6 +476,9 @@
     st_r,
     ge_s,
     ge_r,
+    hop,
+    hop_s,
+    hop_r,
     *sum_scratches,
 ):
     place = Place()
@@ -359,18 +515,44 @@
     ]
     for copy in edges:
         copy.start()
+    half_way = remote(
+        sg_rows.at[pl.ds(2 * ((z + 4) % 8), 2)], sg.at[pl.ds(0, 2), z], a2a_s.at[1], a2a_r.at[4], place.along_z(4)
+    )
+    by_way = [
+        remote(sg_rows.at[pl.ds(2 * ((z + 4) % 8), 2)], hop.at[k], hop_s.at[k], hop_r.at[k], place.along_z(d))
+        for k, d in ((0, 7), (1, 1))
+    ]
+    onward = [
+        remote(hop.at[k], sg.at[pl.ds(0, 2), (z + d) % 8], hop_s.at[2 + k], a2a_r.at[4], place.along_z(5 if k == 0 else 3))
+        for k, d in ((0, 1), (1, 7))
+    ]
+    low = z // 4 == 0
+    relays = ((z + 1) % 8 // 4 == 0, (z + 7) % 8 // 4 == 1)
+
+    @pl.when(place.c == 0)
+    def _():
+        half_way.start()
+
+    @pl.when(jnp.logical_and(place.c == 1, low))
+    def _():
+        by_way[0].start()
+
+    @pl.when(jnp.logical_and(place.c == 1, jnp.logical_not(low)))
+    def _():
+        by_way[1].start()
+
     a2a = {}
-    for d in far:
+    for d in (3, 5, 2, 6, 1, 7):
         peer = (z + d) % 8
         a2a[d] = remote(
-            sg_rows.at[pl.ds(2 * peer, 2)], sg.at[pl.ds(0, 2), z], a2a_s.at[d], a2a_r.at[d], place.along_z(d)
+            sg_rows.at[pl.ds(2 * peer, 2)], sg.at[pl.ds(0, 2), z], a2a_s.at[0], a2a_r.at[d], place.along_z(d)
         )
         a2a[d].start()
     sg[pl.ds(0, 2), z] = sg_rows[pl.ds(2 * z, 2)]
 
-    start = valid[0]
     loads[2].wait()
     loads[5].wait()
+    start = valid[0]
     for f in range(4):
         values = flat(xv[f]).astype(F32)
         values = jnp.where(z * 4 + f >= start, values, 0.0)
@@ -397,6 +579,13 @@
     forward(3, 2)
     forward(5, 2)
     frame = z * 4 + lax.broadcasted_iota(jnp.int32, (256, 256), 0) // 64
+    for k in (0, 1):
+
+        @pl.when(jnp.logical_and(place.c == 1, relays[k]))
+        def _():
+            by_way[k].wait_recv()
+            onward[k].start()
+
     for copy in edges:
         copy.wait()
     for side, row, inside in ((0, 0, h > 0), (1, 9, h < 15)):
@@ -413,7 +602,12 @@
     forward(7, 1)
 
     prior_copy = remote(active.at[:, 3], prior, prior_s, prior_r, place.along_z(1))
-    prior_copy.start()
+
+    @pl.when(z < 7)
+    def _():
+        prior_copy.start()
+
+
     history[pl.ds(0, 2)] = jnp.zeros((2, 64, 256), BF)
     loads[4].wait()
     st = {}
@@ -422,7 +616,7 @@
         for d in far:
             peer = (z + d) % 8
             st[s, d] = remote(
-                strided.at[s, peer], history.at[2 + 2 * z + s], st_s.at[s, d], st_r.at[s, d], place.along_z(d)
+                strided.at[s, peer], history.at[2 + 2 * z + s], st_s, st_r, place.along_z(d)
             )
             st[s, d].start()
         history[2 + 2 * z + s] = strided[s, z]
@@ -434,14 +628,22 @@
         for j in range(3):
             swt[i, j * 256 : (j + 1) * 256] = sw[i, j * 256 : (j + 1) * 256].T
 
-    ahead = {0: remote(sg.at[0, z], sg.at[2, z], next_s.at[0], next_r.at[0], place.along_z(7))}
-    ahead[0].start()
-    for d in (1, 7, 2, 6, 3, 5, 4):
-        a2a[d].wait()
+    ahead = {}
+
+    def send_ahead(d):
         source = (z + 8 - d) % 8
-        ahead[d] = remote(sg.at[0, source], sg.at[2, source], next_s.at[d], next_r.at[d], place.along_z(7))
-        ahead[d].start()
-    send_strided(1)
+        ahead[d] = remote(sg.at[0, source], sg.at[2, source], next_s, next_r, place.along_z(7))
+
+        @pl.when(z > 0)
+        def _():
+            ahead[d].start()
+
+    send_ahead(0)
+    for d in (1, 7, 2, 6, 3, 5):
+        a2a[d].wait_recv()
+        send_ahead(d)
+    half_way.wait_recv()
+    send_ahead(4)
 
 
     def pre_gradient(f, active_gradient):
@@ -463,30 +665,42 @@
     total[base : base + 256] = outer(flat(active[:, 1]), sg_0) + outer(flat(active[:, 3]), sg_1)
     total[base + 256 : base + 512] = outer(flat(active[:, 0]), sg_0) + outer(flat(active[:, 2]), sg_1)
 
-    prior_copy.wait()
-    before = jnp.where(z > 0, flat(prior[...]).astype(F32), 0.0).astype(BF)
-    sum_here = down(flat(active[:, 1]), tw[0]) + down(flat(active[:, 0]), tw[1]) + down(before, tw[2])
-    strided[0] = sum_here.astype(BF).reshape(8, 64, 256)
-    send_strided(0)
-
-    for d in range(8):
-        ahead[d].wait()
+    @pl.when(place.c == 0)
+    def _():
+        half_way.wait_send()
+
+    @pl.when(jnp.logical_and(place.c == 1, low))
+    def _():
+        by_way[0].wait_send()
+
+    @pl.when(jnp.logical_and(place.c == 1, jnp.logical_not(low)))
+    def _():
+        by_way[1].wait_send()
+
+    for k in (0, 1):
+
+        @pl.when(jnp.logical_and(place.c == 1, relays[k]))
+        def _():
+            onward[k].wait_send()
+
+    @pl.when(z > 0)
+    def _():
+        await_bytes(sg.at[2], next_s)
+
+    @pl.when(z < 7)
+    def _():
+        await_bytes(sg.at[2], next_r)
+
+    send_strided(1)
     sg_2 = jnp.where(z < 7, flat(sg[2]).astype(F32), 0.0).astype(BF)
     pre_gradient(3, back(sg_1, tw[0]) + back(sg_2, tw[2]))
-    g_edges = started(
-        [
-            remote(g.at[7], g_edge.at[0], ge_s.at[0], ge_r.at[0], below),
-            remote(g.at[0], g_edge.at[1], ge_s.at[1], ge_r.at[1], above),
-        ]
-    )
-
     for i in range(3):
         total[i * 768 : (i + 1) * 768] += outer(x3[i : i + 8, 3].reshape(512, 768), flat(g[:, 3]))
     total[base + 512 : base + 768] = outer(flat(active[:, 1]), sg_1) + outer(flat(active[:, 3]), sg_2)
-    large = DeviceSum(place, total, 0, gathered_large, sum_scratches[:25])
-    small = DeviceSum(place, total, LARGE, gathered_small, sum_scratches[25:])
-    large.start_core()
-
+    large = DeviceSum(place, total, 0, gathered_large, sum_scratches[:18])
+    small = PlaneSum(place, total, LARGE, gathered_small, sum_scratches[18:25])
+    row_sum = RowSum(place, sum_scratches[25:])
+    large.send_core()
     def clip_gradient(row, gain_sum):
         product = down(g3[row + 2 : row + 4].reshape(512, 768), swt[0])
         for i in (1, 2):
@@ -504,9 +718,30 @@
         return gain_sum
 
     gain_sum = jnp.zeros((1, 256), F32)
+    large.send_first()
+    @pl.when(z < 7)
+    def _():
+        prior_copy.wait_send()
+
+    @pl.when(z > 0)
+    def _():
+        prior_copy.wait_recv()
+
+    before = jnp.where(z > 0, flat(prior[...]).astype(F32), 0.0).astype(BF)
+    sum_here = down(flat(active[:, 1]), tw[0]) + down(flat(active[:, 0]), tw[1]) + down(before, tw[2])
+    strided[0] = sum_here.astype(BF).reshape(8, 64, 256)
+    send_strided(0)
     gain_sum = clip_gradient(2, gain_sum)
+    large.relay_first()
     gain_sum = clip_gradient(4, gain_sum)
-    large.start_first()
+    large.send_second()
+    g_edges = started(
+        [
+            remote(g.at[7], g_edge.at[0], ge_s.at[0], ge_r.at[0], below),
+            remote(g.at[0], g_edge.at[1], ge_s.at[1], ge_r.at[1], above),
+        ]
+    )
+    large.start_z()
     finished(g_edges)
     for side, row, inside in ((0, 0, h > 0), (1, 9, h < 15)):
         values = flat(g_edge[side]).astype(F32)
@@ -516,42 +751,44 @@
         g3[row, :, :, 256:512] = values.astype(BF).reshape(4, 64, 256)
         g3[row, :, :, 512:768] = left.astype(BF).reshape(4, 64, 256)
     gain_sum = clip_gradient(0, gain_sum)
-    gain_sum = clip_gradient(6, gain_sum)
-    total[15 * 256 : 16 * 256] = jnp.zeros((256, 256), F32)
-    total[15 * 256 : 15 * 256 + 1] = gain_sum
-
-    for s in (1, 0):
-        for d in far:
-            st[s, d].wait()
+    await_bytes(history.at[pl.ds(0, 14)], st_r)
     base = 12 * 256
     cot_all = flat(cv[0:16])
     for k in range(3):
         total[base + k * 256 : base + (k + 1) * 256] = outer(flat(history[2 - k : 18 - k]), cot_all)
-    small.start_core()
-    large.start_second()
+    total[15 * 256 : 16 * 256] = jnp.zeros((256, 256), F32)
+    small.send_core()
+    gain_sum = clip_gradient(6, gain_sum)
+    row_sum.send(0, jnp.broadcast_to(gain_sum, (8, 256)))
+    small.send_plane()
+    large.start_z_back()
     for f in (0, 8):
         sum_here = flat(history[f + 2 : f + 10]).astype(F32)
         for k in range(3):
             sum_here = sum_here + down(flat(history[f + 2 - k : f + 10 - k]), mw[k])
         enc[f : f + 8] = sum_here.astype(BF).reshape(8, 64, 256)
-    small.start_first()
-    large.start_z()
-    small.start_second()
-    large.start_z_back()
-    small.start_z_at_once()
-    large.finish_z_back()
-    large.start_second_back()
-    small.finish_z_at_once()
-    small.start_second_back()
-    large.start_first_back()
-    small.start_first_back()
-    small.start_core_back()
-    large.start_core_back()
+    row_sum.step(0)
+    large.start_back()
+    row_sum.step(1)
+    small.start_z()
+    large.back_second(0)
+    large.back_first(0)
+    large.back_second(1)
+    row_sum.step(2)
+    large.back_first(1)
+    large.back_first(3)
+    large.back_first(2)
+    small.start_back()
+    large.back_far()
+    gain_total[...] = row_sum.take(3)
+    small.core_back()
+    await_bytes(sg_rows.at[pl.ds(0, 12)], a2a_s.at[0])
+    await_bytes(strided.at[:, pl.ds(0, 7)], st_s)
+    large.finish()
     small.finish()
-    large.finish()
-
-
-def finish_kernel(scale, enc, vg, large, small, encoded, video_gradient, spatial, temporal, mix, gain_out, ws, wt, wm, wg, sems):
+
+
+def finish_kernel(scale, enc, vg, large, small, gain_total, encoded, video_gradient, spatial, temporal, mix, gain_out, ws, wt, wm, wg, sems):
     copies = started(
         [
             pltpu.make_async_copy(vg, video_gradient, sems.at[0]),
@@ -564,7 +801,7 @@
     for i in range(3):
         wt[i] = large[(9 + i) * 256 : (10 + i) * 256].astype(F32) * scale
         wm[i] = small[i * 256 : (i + 1) * 256].astype(F32) * scale
-    wg[...] = small[3 * 256 : 3 * 256 + 16].astype(F32)[0:1] * scale
+    wg[...] = gain_total[0:1] * scale
     copies += started(
         [
             pltpu.make_async_copy(wt, temporal, sems.at[3]),
@@ -586,9 +823,10 @@
             jax.ShapeDtypeStruct((4, 8, 64, 256), BF),
             jax.ShapeDtypeStruct((LARGE, 256), BF),
             jax.ShapeDtypeStruct((SMALL, 256), BF),
+            jax.ShapeDtypeStruct((8, 256), F32),
         ),
         in_specs=[pl.BlockSpec(memory_space=pltpu.SMEM)] + [anywhere] * 6,
-        out_specs=(here,) * 4,
+        out_specs=(here,) * 5,
         scratch_shapes=[
             vmem((4, 8, 64, 256), BF),
             vmem((3, 768, 256), BF),
@@ -614,19 +852,21 @@
             dma((6,)),
             dma((2,)),
             dma((2,)),
-            dma((8,)),
-            dma((8,)),
-            dma((8,)),
+            dma((2,)),
             dma((8,)),
             dma,
             dma,
-            dma((2, 8)),
-            dma((2, 8)),
+            dma,
+            dma,
+            dma,
+            dma,
             dma((2,)),
             dma((2,)),
+            vmem((2, 2, 64, 256), BF),
+            dma((4,)),
+            dma((2,)),
         ]
-        + sum_scratch(LARGE, False)
-        + sum_scratch(SMALL, True),
+        + sum(sum_scratch(), []),
         compiler_params=pltpu.CompilerParams(collective_id=0, has_side_effects=True, vmem_limit_bytes=VMEM_LIMIT),
         name="down_block",
     )(
@@ -647,7 +887,7 @@
             jax.ShapeDtypeStruct((3, 256, 256), F32),
             jax.ShapeDtypeStruct((1, 256), F32),
         ),
-        in_specs=[here] * 4,
+        in_specs=[here] * 5,
         out_specs=(anywhere,) * 6,
         scratch_shapes=[
             vmem((9, 256, 256), F32),

time: 86.4 us -> 79.5 us (0.920)
  Pallas kernels: 84.9 us -> 78 us
    pallas_call x1, Pallas kernels: 82.4 us -> 75.5 us  [block_call(): pl.pallas_call(block_kernel, out_shape=(jax.ShapeDtypeStruct((16, 64, 256...]
where the time goes in v1:
time: 79.5 us; the launch traced here: 79.4 us
  Pallas kernels  78 us (98%)
  between operations  1.45 us (2%)
    pallas_call x1, Pallas kernels, block_call(): pl.pallas_call(block_kernel, out_shape=(jax.ShapeDtypeStruct((16, 64, 256...  75.5 us
    pallas_call x1, Pallas kernels, block_call(): pl.pallas_call(functools.partial(finish_kernel, scale), out_shape=(jax.Sh...  2.49 us

profile of v1, /device:TPU:1, one launch (start us, length us, event | category | flops | bytes accessed | tf_op | source)
XLA Modules:
  0.0 79.4 jit_solution(3646399094511641023)
XLA Ops:
  1.3 75.5 %down_block.1 = (bf16[16,64,256]{2,1,0:T(8,128)(2,1)S(1)}, bf16[4,8,64,256]{3,2,1,0:T(8,128)(2,1)S(1)}, bf16[3072,256]{1,0:T(8,128)(2,1)S(1)}, bf16[1024,256]{1,0:T(8,128)(2,1)S(1)}, f32[8,256]{1,0:T(8,128)S(1)}) custom-call(s32[1]{0:T(128)S(6)} %copy.14.valid, f32[1,256]{1,0:T(1,128)} %bitcast.13, bf16[4,8,64,256]{3,2,1,0:T(8,128)(2,1)} %bitcast.11, ...), custom_call_target="tpu_custom_call" | custom-call | tf_op jit(solution)/shard_map/down_block/pallas_call | solution.py:819
  76.8 2.5 %write_out.1 = (bf16[16,64,256]{2,1,0:T(8,128)(2,1)}, bf16[4,8,64,256]{3,2,1,0:T(8,128)(2,1)}, f32[9,256,256]{2,1,0:T(8,128)}, f32[3,256,256]{2,1,0:T(8,128)}, f32[3,256,256]{2,1,0:T(8,128)}, /*index=5*/f32[1,256]{1,0:T(1,128)}) custom-call(bf16[16,64,256]{2,1,0:T(8,128)(2,1)S(1)} %get-tuple-element.17.enc, ...), custom_call_target="tpu_custom_call" | custom-call | tf_op jit(solution)/shard_map/write_out/pallas_call | solution.py:880

commit v2 on v1

--- a/solution.py
+++ b/solution.py
@@ -12,7 +12,7 @@
 BF = jnp.bfloat16
 F32 = jnp.float32
 LARGE = 12 * 256
-SMALL = 4 * 256
+SMALL = 3 * 256
 VMEM_LIMIT = 46 << 20
 
 
@@ -280,20 +280,20 @@
     def __init__(self, place, total, base, gathered, scratch):
         self.place, self.total, self.base, self.gathered = place, total, base, gathered
         self.halved, self.landed_c, self.held, self.landed, self.landed_z, self.sent, self.received = scratch
-        rows = gathered.shape[0]
-        self.half, self.n = rows // 2, rows // 32
+        self.n = gathered.shape[1]
+        self.half = 16 * self.n
         self.mine = place.c * self.half
 
     def send_core(self):
         other = pl.multiple_of(self.base + (1 - self.place.c) * self.half, 16)
-        self.halved[...] = self.total[pl.ds(other, self.half), :].astype(BF)
+        self.halved[...] = self.total[pl.ds(other, self.half), :].reshape(16, self.n, 256).astype(BF)
         remote(self.halved, self.landed_c, self.sent.at[0], self.received.at[0], self.place.across()).start()
 
     def send_plane(self):
         await_bytes(self.landed_c, self.received.at[0])
         own = pl.multiple_of(self.base + self.mine, 16)
-        value = self.total[pl.ds(own, self.half), :] + self.landed_c[...].astype(F32)
-        self.held[...] = value.astype(BF).reshape(16, self.n, 256)
+        value = self.total[pl.ds(own, self.half), :].reshape(16, self.n, 256) + self.landed_c[...].astype(F32)
+        self.held[...] = value.astype(BF)
         for d in PLANE:
             remote(
                 self.held.at[(self.place.h + d) % 16],
@@ -320,15 +320,15 @@
         sum_here = self.landed_z[0].astype(F32)
         for k in range(1, 8):
             sum_here = sum_here + self.landed_z[k].astype(F32)
-        rows = pl.ds(pl.multiple_of(self.mine + self.place.h * self.n, 16), self.n)
-        self.gathered[rows, :] = sum_here.astype(BF)
-        at = self.gathered.at[rows]
+        mine = self.place.c * 16 + self.place.h
+        self.gathered[mine] = sum_here.astype(BF)
+        at = self.gathered.at[mine]
         for d in PLANE:
             remote(at, at, self.sent.at[3], self.received.at[3], self.place.in_plane(d)).start()
 
     def core_back(self):
         await_bytes(self.landed, self.received.at[3])
-        at = self.gathered.at[pl.ds(pl.multiple_of(self.mine, 16), self.half)]
+        at = self.gathered.at[pl.ds(self.place.c * 16, 16)]
         remote(at, at, self.sent.at[4], self.received.at[4], self.place.across()).start()
 
     def finish(self):
@@ -393,8 +393,8 @@
         dma,
     ]
     small = [
-        vmem((SMALL // 2, 256), BF),
-        vmem((SMALL // 2, 256), BF),
+        vmem((16, n, 256), BF),
+        vmem((16, n, 256), BF),
         vmem((16, n, 256), BF),
         vmem((15, n, 256), BF),
         vmem((8, n, 256), BF),
@@ -694,6 +694,12 @@
     send_strided(1)
     sg_2 = jnp.where(z < 7, flat(sg[2]).astype(F32), 0.0).astype(BF)
     pre_gradient(3, back(sg_1, tw[0]) + back(sg_2, tw[2]))
+    g_edges = started(
+        [
+            remote(g.at[7], g_edge.at[0], ge_s.at[0], ge_r.at[0], below),
+            remote(g.at[0], g_edge.at[1], ge_s.at[1], ge_r.at[1], above),
+        ]
+    )
     for i in range(3):
         total[i * 768 : (i + 1) * 768] += outer(x3[i : i + 8, 3].reshape(512, 768), flat(g[:, 3]))
     total[base + 512 : base + 768] = outer(flat(active[:, 1]), sg_1) + outer(flat(active[:, 3]), sg_2)
@@ -735,13 +741,6 @@
     large.relay_first()
     gain_sum = clip_gradient(4, gain_sum)
     large.send_second()
-    g_edges = started(
-        [
-            remote(g.at[7], g_edge.at[0], ge_s.at[0], ge_r.at[0], below),
-            remote(g.at[0], g_edge.at[1], ge_s.at[1], ge_r.at[1], above),
-        ]
-    )
-    large.start_z()
     finished(g_edges)
     for side, row, inside in ((0, 0, h > 0), (1, 9, h < 15)):
         values = flat(g_edge[side]).astype(F32)
@@ -751,34 +750,34 @@
         g3[row, :, :, 256:512] = values.astype(BF).reshape(4, 64, 256)
         g3[row, :, :, 512:768] = left.astype(BF).reshape(4, 64, 256)
     gain_sum = clip_gradient(0, gain_sum)
+    gain_sum = clip_gradient(6, gain_sum)
+    large.start_z()
+    row_sum.send(0, jnp.broadcast_to(gain_sum, (8, 256)))
     await_bytes(history.at[pl.ds(0, 14)], st_r)
     base = 12 * 256
     cot_all = flat(cv[0:16])
     for k in range(3):
         total[base + k * 256 : base + (k + 1) * 256] = outer(flat(history[2 - k : 18 - k]), cot_all)
-    total[15 * 256 : 16 * 256] = jnp.zeros((256, 256), F32)
     small.send_core()
-    gain_sum = clip_gradient(6, gain_sum)
-    row_sum.send(0, jnp.broadcast_to(gain_sum, (8, 256)))
-    small.send_plane()
-    large.start_z_back()
     for f in (0, 8):
         sum_here = flat(history[f + 2 : f + 10]).astype(F32)
         for k in range(3):
             sum_here = sum_here + down(flat(history[f + 2 - k : f + 10 - k]), mw[k])
         enc[f : f + 8] = sum_here.astype(BF).reshape(8, 64, 256)
     row_sum.step(0)
-    large.start_back()
+    small.send_plane()
+    large.start_z_back()
     row_sum.step(1)
     small.start_z()
+    large.start_back()
+    row_sum.step(2)
     large.back_second(0)
     large.back_first(0)
     large.back_second(1)
-    row_sum.step(2)
+    small.start_back()
     large.back_first(1)
     large.back_first(3)
     large.back_first(2)
-    small.start_back()
     large.back_far()
     gain_total[...] = row_sum.take(3)
     small.core_back()
@@ -797,18 +796,19 @@
     )
     for i in range(9):
         ws[i] = large[i * 256 : (i + 1) * 256].astype(F32) * scale
-    copies += started([pltpu.make_async_copy(ws, spatial, sems.at[2])])
+        pltpu.make_async_copy(ws.at[i], spatial.at[i], sems.at[2]).start()
     for i in range(3):
         wt[i] = large[(9 + i) * 256 : (10 + i) * 256].astype(F32) * scale
-        wm[i] = small[i * 256 : (i + 1) * 256].astype(F32) * scale
+    copies += started([pltpu.make_async_copy(wt, temporal, sems.at[3])])
+    wm[...] = (small[...].astype(F32) * scale).reshape(3, 256, 256)
     wg[...] = gain_total[0:1] * scale
     copies += started(
         [
-            pltpu.make_async_copy(wt, temporal, sems.at[3]),
             pltpu.make_async_copy(wm, mix, sems.at[4]),
             pltpu.make_async_copy(wg, gain_out, sems.at[5]),
         ]
     )
+    pltpu.make_async_copy(ws, spatial, sems.at[2]).wait()
     finished(copies)
 
 
@@ -822,7 +822,7 @@
             jax.ShapeDtypeStruct((16, 64, 256), BF),
             jax.ShapeDtypeStruct((4, 8, 64, 256), BF),
             jax.ShapeDtypeStruct((LARGE, 256), BF),
-            jax.ShapeDtypeStruct((SMALL, 256), BF),
+            jax.ShapeDtypeStruct((32, SMALL // 32, 256), BF),
             jax.ShapeDtypeStruct((8, 256), F32),
         ),
         in_specs=[pl.BlockSpec(memory_space=pltpu.SMEM)] + [anywhere] * 6,

time: 79.5 us -> 74.6 us (0.938)
  Pallas kernels: 78 us -> 73.1 us
    pallas_call x1, Pallas kernels: 75.5 us -> 70.6 us  [block_call(): pl.pallas_call(block_kernel, out_shape=(jax.ShapeDtypeStruct((16, 64, 256...]
where the time goes in v2:
time: 74.6 us; the launch traced here: 74.5 us
  Pallas kernels  73.1 us (98%)
  between operations  1.45 us (2%)
    pallas_call x1, Pallas kernels, block_call(): pl.pallas_call(block_kernel, out_shape=(jax.ShapeDtypeStruct((16, 64, 256...  70.6 us
    pallas_call x1, Pallas kernels, block_call(): pl.pallas_call(functools.partial(finish_kernel, scale), out_shape=(jax.Sh...  2.49 us

profile of v2, /device:TPU:1, one launch (start us, length us, event | category | flops | bytes accessed | tf_op | source)
XLA Modules:
  0.0 74.5 jit_solution(12983412562625803469)
XLA Ops:
  1.3 70.6 %down_block.1 = (bf16[16,64,256]{2,1,0:T(8,128)(2,1)S(1)}, bf16[4,8,64,256]{3,2,1,0:T(8,128)(2,1)S(1)}, bf16[3072,256]{1,0:T(8,128)(2,1)S(1)}, bf16[32,24,256]{2,1,0:T(8,128)(2,1)S(1)}, f32[8,256]{1,0:T(8,128)S(1)}) custom-call(s32[1]{0:T(128)S(6)} %copy.14.valid, f32[1,256]{1,0:T(1,128)} %bitcast.13, bf16[4,8,64,256]{3,2,1,0:T(8,128)(2,1)} %bitcast.11, ...), custom_call_target="tpu_custom_call" | custom-call | tf_op jit(solution)/shard_map/down_block/pallas_call | solution.py:819
  71.9 2.5 %write_out.1 = (bf16[16,64,256]{2,1,0:T(8,128)(2,1)}, bf16[4,8,64,256]{3,2,1,0:T(8,128)(2,1)}, f32[9,256,256]{2,1,0:T(8,128)}, f32[3,256,256]{2,1,0:T(8,128)}, f32[3,256,256]{2,1,0:T(8,128)}, /*index=5*/f32[1,256]{1,0:T(1,128)}) custom-call(bf16[16,64,256]{2,1,0:T(8,128)(2,1)S(1)} %get-tuple-element.17.enc, ...), custom_call_target="tpu_custom_call" | custom-call | tf_op jit(solution)/shard_map/write_out/pallas_call | solution.py:880

commit v3 on v2

--- a/solution.py
+++ b/solution.py
@@ -603,10 +603,6 @@
 
     prior_copy = remote(active.at[:, 3], prior, prior_s, prior_r, place.along_z(1))
 
-    @pl.when(z < 7)
-    def _():
-        prior_copy.start()
-
 
     history[pl.ds(0, 2)] = jnp.zeros((2, 64, 256), BF)
     loads[4].wait()
@@ -639,7 +635,15 @@
             ahead[d].start()
 
     send_ahead(0)
-    for d in (1, 7, 2, 6, 3, 5):
+    for d in (1, 7, 2, 6):
+        a2a[d].wait_recv()
+        send_ahead(d)
+
+    @pl.when(z < 7)
+    def _():
+        prior_copy.start()
+
+    for d in (3, 5):
         a2a[d].wait_recv()
         send_ahead(d)
     half_way.wait_recv()
@@ -691,7 +695,6 @@
     def _():
         await_bytes(sg.at[2], next_r)
 
-    send_strided(1)
     sg_2 = jnp.where(z < 7, flat(sg[2]).astype(F32), 0.0).astype(BF)
     pre_gradient(3, back(sg_1, tw[0]) + back(sg_2, tw[2]))
     g_edges = started(
@@ -707,6 +710,7 @@
     small = PlaneSum(place, total, LARGE, gathered_small, sum_scratches[18:25])
     row_sum = RowSum(place, sum_scratches[25:])
     large.send_core()
+    send_strided(1)
     def clip_gradient(row, gain_sum):
         product = down(g3[row + 2 : row + 4].reshape(512, 768), swt[0])
         for i in (1, 2):
@@ -771,8 +775,8 @@
     small.start_z()
     large.start_back()
     row_sum.step(2)
+    large.back_first(0)
     large.back_second(0)
-    large.back_first(0)
     large.back_second(1)
     small.start_back()
     large.back_first(1)

time: 74.6 us -> 73.6 us (0.987)
  Pallas kernels: 73.1 us -> 72 us
    pallas_call x1, Pallas kernels: 70.6 us -> 69.6 us  [block_call(): pl.pallas_call(block_kernel, out_shape=(jax.ShapeDtypeStruct((16, 64, 256...]
where the time goes in v3:
time: 73.6 us; the launch traced here: 73.5 us
  Pallas kernels  72 us (98%)
  between operations  1.45 us (2%)
    pallas_call x1, Pallas kernels, block_call(): pl.pallas_call(block_kernel, out_shape=(jax.ShapeDtypeStruct((16, 64, 256...  69.6 us
    pallas_call x1, Pallas kernels, block_call(): pl.pallas_call(functools.partial(finish_kernel, scale), out_shape=(jax.Sh...  2.49 us

profile of v3, /device:TPU:1, one launch (start us, length us, event | category | flops | bytes accessed | tf_op | source)
XLA Modules:
  0.0 73.5 jit_solution(9761173855145186382)
XLA Ops:
  1.3 69.6 %down_block.1 = (bf16[16,64,256]{2,1,0:T(8,128)(2,1)S(1)}, bf16[4,8,64,256]{3,2,1,0:T(8,128)(2,1)S(1)}, bf16[3072,256]{1,0:T(8,128)(2,1)S(1)}, bf16[32,24,256]{2,1,0:T(8,128)(2,1)S(1)}, f32[8,256]{1,0:T(8,128)S(1)}) custom-call(s32[1]{0:T(128)S(6)} %copy.14.valid, f32[1,256]{1,0:T(1,128)} %bitcast.13, bf16[4,8,64,256]{3,2,1,0:T(8,128)(2,1)} %bitcast.11, ...), custom_call_target="tpu_custom_call" | custom-call | tf_op jit(solution)/shard_map/down_block/pallas_call | solution.py:823
  70.8 2.5 %write_out.1 = (bf16[16,64,256]{2,1,0:T(8,128)(2,1)}, bf16[4,8,64,256]{3,2,1,0:T(8,128)(2,1)}, f32[9,256,256]{2,1,0:T(8,128)}, f32[3,256,256]{2,1,0:T(8,128)}, f32[3,256,256]{2,1,0:T(8,128)}, /*index=5*/f32[1,256]{1,0:T(1,128)}) custom-call(bf16[16,64,256]{2,1,0:T(8,128)(2,1)S(1)} %get-tuple-element.17.enc, ...), custom_call_target="tpu_custom_call" | custom-call | tf_op jit(solution)/shard_map/write_out/pallas_call | solution.py:884
